TPU v7x, 32 devices: a whole 2x2x4 slice. The times are simulated.
32 devices in a mesh: dp: 8 (over y, x, core), tensor: 4 (over z).
Axes of the slice: x: 2, y: 2, z: 4, core: 2. Of those that a mesh axis runs over, the one named last changes fastest.
Arguments:
- block_in: float32 [4096, 1024], P(('dp', 'tensor')), may hold values from -6 to 6
- cotangent: float32 [4096, 1024], P(('dp', 'tensor')), may hold values from -6 to 6
- routes: int32 [4096, 8], P('dp'), may hold values from 0 to 15, all different within a row; in each aligned block of 512 rows (0 to 511, 512 to 1023, ...) at most 288 rows name the same one
- gate_weights: float32 [4096, 8], P('dp'), may hold values from 0.02 to 0.3
- norm_gains: float32 [2, 1024], P(None, 'dp'), may hold values from 0.5 to 1.5
- attention_weight: float32 [4, 1024, 512], P(None, 'dp', 'tensor'), may hold values from -0.1875 to 0.1875
- output_weight: float32 [2, 1024, 512], P(None, 'dp', 'tensor'), may hold values from -0.75 to 0.75
- w_gate_up: float32 [16, 2, 1024, 512], P(None, None, 'dp', 'tensor'), may hold values from -0.1875 to 0.1875
- w_down: float32 [16, 1024, 512], P(None, 'dp', 'tensor'), may hold values from -0.75 to 0.75
- m_gains: float32 [2, 1024], P(None, 'dp'), may hold values from -128 to 128
- v_gains: float32 [2, 1024], P(None, 'dp'), may hold values from 100 to 10000
- attention_first_moment: float32 [4, 1024, 512], P(None, 'dp', 'tensor'), may hold values from -12 to 12
- attention_second_moment: float32 [4, 1024, 512], P(None, 'dp', 'tensor'), may hold values from 1 to 100
- output_first_moment: float32 [2, 1024, 512], P(None, 'dp', 'tensor'), may hold values from -16 to 16
- output_second_moment: float32 [2, 1024, 512], P(None, 'dp', 'tensor'), may hold values from 1 to 100
- m_gate_up: float32 [16, 2, 1024, 512], P(None, None, 'dp', 'tensor'), may hold values from -32 to 32
- v_gate_up: float32 [16, 2, 1024, 512], P(None, None, 'dp', 'tensor'), may hold values from 10 to 1000
- m_down: float32 [16, 1024, 512], P(None, 'dp', 'tensor'), may hold values from -12 to 12
- v_down: float32 [16, 1024, 512], P(None, 'dp', 'tensor'), may hold values from 1 to 100
Outputs:
- block_out: float32 [4096, 1024], P(('dp', 'tensor'))
- input_grad: float32 [4096, 1024], P(('dp', 'tensor'))
- grad_gains: float32 [2, 1024], P(None, 'dp')
- grad_attn: float32 [4, 1024, 512], P(None, 'dp', 'tensor')
- grad_out: float32 [2, 1024, 512], P(None, 'dp', 'tensor')
- grad_gate_up: float32 [16, 2, 1024, 512], P(None, None, 'dp', 'tensor')
- grad_down: float32 [16, 1024, 512], P(None, 'dp', 'tensor')
- new_gains: float32 [2, 1024], P(None, 'dp')
- new_attn: float32 [4, 1024, 512], P(None, 'dp', 'tensor')
- new_out: float32 [2, 1024, 512], P(None, 'dp', 'tensor')
- new_gate_up: float32 [16, 2, 1024, 512], P(None, None, 'dp', 'tensor')
- new_down: float32 [16, 1024, 512], P(None, 'dp', 'tensor')
- new_m_gains: float32 [2, 1024], P(None, 'dp')
- new_v_gains: float32 [2, 1024], P(None, 'dp')
- new_m_attn: float32 [4, 1024, 512], P(None, 'dp', 'tensor')
- new_v_attn: float32 [4, 1024, 512], P(None, 'dp', 'tensor')
- new_m_out: float32 [2, 1024, 512], P(None, 'dp', 'tensor')
- new_v_out: float32 [2, 1024, 512], P(None, 'dp', 'tensor')
- new_m_gate_up: float32 [16, 2, 1024, 512], P(None, None, 'dp', 'tensor')
- new_v_gate_up: float32 [16, 2, 1024, 512], P(None, None, 'dp', 'tensor')
- new_m_down: float32 [16, 1024, 512], P(None, 'dp', 'tensor')
- new_v_down: float32 [16, 1024, 512], P(None, 'dp', 'tensor')
Inputs may be any that keep to these rules, and one draw needn't show every extreme that they name: `routes`: each row names 8 different experts. Within each aligned block of 512 rows no expert is named by more than 288 rows, and in some block one expert is named by exactly 288 rows.
All inputs are finite; a program needn't handle non-finite values.
Results may differ from a plain program's by a relative error of at most 0.015.
The roundings to bfloat16 on the way count: a program that leaves them out, or rounds other values in their place, can miss the bound.
Values may be sent and summed in bfloat16 or wider, within the bound.
A program may use at most 192 MiB of HBM per device.

v0:
```python
import jax
import jax.numpy as jnp
from jax import lax
from jax.sharding import PartitionSpec as P

HEAD_SIZE = 64
SEQ = 512
STEP = 3
norm_eps = 1e-05
beta_one = 0.9
beta_two = 0.95
adam_eps = 1e-08
rate_matrix = 0.02
rate_gain = 0.2
decay_matrix = 0.1
rope_base = 10000.0


def rope_tables(length, width):
    half_width = width // 2
    frequency = rope_base ** (-(2.0 * jnp.arange(half_width, dtype=jnp.float32)) / width)
    angles = jnp.arange(length, dtype=jnp.float32)[:, None] * frequency[None, :]
    return (jnp.cos(angles)[:, None, :], jnp.sin(angles)[:, None, :])


def rotate(vectors, cos_table, sine_table):
    half_width = vectors.shape[-1] // 2
    lower_half = vectors[..., :half_width]
    upper_half = vectors[..., half_width:]
    return jnp.concatenate(
        [
            lower_half * cos_table - upper_half * sine_table,
            upper_half * cos_table + lower_half * sine_table,
        ],
        axis=-1,
    )


def unrotate(vectors, cos_table, sine_table):
    half_width = vectors.shape[-1] // 2
    lower_half = vectors[..., :half_width]
    upper_half = vectors[..., half_width:]
    return jnp.concatenate(
        [
            lower_half * cos_table + upper_half * sine_table,
            upper_half * cos_table - lower_half * sine_table,
        ],
        axis=-1,
    )


def causal_scores(queries, keys_rot):
    scale = queries.shape[-1] ** (-0.5)
    scores = (
        jnp.einsum("jqgh,kgh->jgqk", queries, keys_rot, preferred_element_type=jnp.float32) * scale
    )
    length = scores.shape[-1]
    allowed = lax.broadcasted_iota(jnp.int32, (length, length), 0) >= lax.broadcasted_iota(
        jnp.int32, (length, length), 1
    )
    return jnp.where(allowed, scores, -jnp.inf)


def attend(items):
    queries, keys_rot, values = items
    scores = causal_scores(queries, keys_rot)
    log_totals = jax.nn.logsumexp(scores, axis=-1)
    softmax_b = jnp.exp(scores - log_totals[..., None]).astype(jnp.bfloat16)
    attended = jnp.einsum(
        "jgqk,kgh->jqgh", softmax_b, values, preferred_element_type=jnp.float32
    ).astype(jnp.bfloat16)
    return (attended, log_totals)


def attend_back(items):
    queries, keys_rot, values, attended, log_totals, attended_cot = items
    scale = queries.shape[-1] ** (-0.5)
    scores = causal_scores(queries, keys_rot)
    softmax_f = jnp.exp(scores - log_totals[..., None])
    softmax_b = softmax_f.astype(jnp.bfloat16)
    value_cot = jnp.einsum(
        "jgqk,jqgh->kgh", softmax_b, attended_cot, preferred_element_type=jnp.float32
    )
    weight_cot = jnp.einsum(
        "jqgh,kgh->jgqk", attended_cot, values, preferred_element_type=jnp.float32
    )
    row_dots = jnp.einsum(
        "jqgh,jqgh->jgq", attended_cot, attended, preferred_element_type=jnp.float32
    )
    score_cot = (softmax_f * (weight_cot - row_dots[..., None])).astype(jnp.bfloat16)
    query_cot = (
        jnp.einsum("jgqk,kgh->jqgh", score_cot, keys_rot, preferred_element_type=jnp.float32)
        * scale
    )
    key_cot = (
        jnp.einsum("jgqk,jqgh->kgh", score_cot, queries, preferred_element_type=jnp.float32) * scale
    )
    return (query_cot, key_cot, value_cot)


def adamw_update(weight, moment_one, moment_two, gradient, rate, decay):
    new_one = beta_one * moment_one + (1.0 - beta_one) * gradient
    new_two = beta_two * moment_two + (1.0 - beta_two) * gradient * gradient
    corrected_one = new_one / (1.0 - beta_one**STEP)
    corrected_two = new_two / (1.0 - beta_two**STEP)
    new_weight = weight - rate * (
        corrected_one / (jnp.sqrt(corrected_two) + adam_eps) + decay * weight
    )
    return (new_weight, new_one, new_two)


def local(
    block_in,
    cotangent,
    routes,
    gate_weights,
    norm_gains,
    attention_weight,
    output_weight,
    w_gate_up,
    w_down,
    m_gains,
    v_gains,
    attention_first_moment,
    attention_second_moment,
    output_first_moment,
    output_second_moment,
    m_gate_up,
    v_gate_up,
    m_down,
    v_down,
):
    bf = jnp.bfloat16
    f32 = jnp.float32
    tok_count = routes.shape[0]
    seq_count = tok_count // SEQ
    width = block_in.shape[1]
    experts = w_gate_up.shape[0]
    rows = w_gate_up.shape[2]
    units = w_gate_up.shape[3]
    cols = attention_weight.shape[2]
    kv_count = cols // HEAD_SIZE
    gains_all = lax.all_gather(norm_gains.astype(bf), "dp", axis=1, tiled=True)
    attn_rows = jnp.concatenate([attention_weight, output_weight], axis=0)
    attn_rows = attn_rows.astype(bf).transpose(1, 0, 2).reshape(rows, 6 * cols)
    attn_all = lax.all_gather(attn_rows, "dp", axis=0, tiled=True)
    proj_all = attn_all[:, : 4 * cols]
    out_all = attn_all[:, 4 * cols :]
    gate_up_rows = w_gate_up.astype(bf).transpose(2, 1, 0, 3).reshape(rows, 2 * experts * units)
    down_rows = w_down.astype(bf).transpose(1, 0, 2).reshape(rows, experts * units)
    cos_table, sine_table = rope_tables(SEQ, HEAD_SIZE)
    gain_one = gains_all[0].astype(f32)
    gain_two = gains_all[1].astype(f32)
    inv_one = lax.rsqrt(jnp.mean(block_in * block_in, axis=1, keepdims=True) + norm_eps)
    normed_one = (block_in * inv_one * gain_one).astype(bf)
    tokens_one = lax.all_gather(normed_one, "tensor", axis=0, tiled=True)
    gate_up_all = lax.all_gather(gate_up_rows, "dp", axis=0, tiled=True)
    down_all = lax.all_gather(down_rows, "dp", axis=0, tiled=True)
    cot_all = lax.all_gather(cotangent.astype(bf), "tensor", axis=0, tiled=True)
    projected = jnp.dot(tokens_one, proj_all, preferred_element_type=f32)
    head_vals = projected.reshape(seq_count, SEQ, 4, kv_count, HEAD_SIZE).transpose(2, 0, 1, 3, 4)
    queries = rotate(head_vals[0:2], cos_table, sine_table).astype(bf).transpose(1, 0, 2, 3, 4)
    keys_rot = rotate(head_vals[2], cos_table, sine_table).astype(bf)
    values = head_vals[3].astype(bf)
    attended, log_totals = lax.map(attend, (queries, keys_rot, values))
    attended_flat = attended.transpose(0, 2, 1, 3, 4).reshape(tok_count, 2 * cols)
    partial_value = jnp.dot(attended_flat, out_all.T, preferred_element_type=f32).astype(bf)
    residual = block_in + lax.psum_scatter(
        partial_value, "tensor", scatter_dimension=0, tiled=True
    ).astype(f32)
    inv_two = lax.rsqrt(jnp.mean(residual * residual, axis=1, keepdims=True) + norm_eps)
    normed_two = (residual * inv_two * gain_two).astype(bf)
    tokens_two = lax.all_gather(normed_two, "tensor", axis=0, tiled=True)
    expert_ids = jnp.arange(experts, dtype=jnp.int32)[None, None, :]
    token_weight = jnp.sum(
        jnp.where(routes[:, :, None] == expert_ids, gate_weights[:, :, None], 0.0), axis=1
    )
    weight_wide = jnp.broadcast_to(token_weight[:, :, None], (tok_count, experts, units)).reshape(
        tok_count, experts * units
    )
    half = experts * units
    gate_up = jnp.dot(tokens_two, gate_up_all, preferred_element_type=f32)
    gate_vals = gate_up[:, :half]
    up_vals = gate_up[:, half:]
    sigmoid_vals = jax.nn.sigmoid(gate_vals)
    hidden = (gate_vals * sigmoid_vals * up_vals * weight_wide).astype(bf)
    hidden_cot = jnp.dot(cot_all, down_all, preferred_element_type=f32) * weight_wide
    gate_cot = (
        hidden_cot * up_vals * sigmoid_vals * (1.0 + gate_vals * (1.0 - sigmoid_vals))
    ).astype(bf)
    up_cot = (hidden_cot * gate_vals * sigmoid_vals).astype(bf)
    both_cot = jnp.concatenate([gate_cot, up_cot], axis=1)
    back_sum = lax.dot_general(
        both_cot, gate_up_all, (((1,), (1,)), ((), ())), preferred_element_type=f32
    ).astype(bf)
    normed_two_cot = lax.psum_scatter(back_sum, "tensor", scatter_dimension=0, tiled=True).astype(
        f32
    )
    down_local = lax.dot_general(
        cot_all, hidden, (((0,), (0,)), ((), ())), preferred_element_type=f32
    ).astype(bf)
    gate_up_local = lax.dot_general(
        tokens_two, both_cot, (((0,), (0,)), ((), ())), preferred_element_type=f32
    ).astype(bf)
    mixture = lax.dot_general(
        hidden, down_all, (((1,), (1,)), ((), ())), preferred_element_type=f32
    ).astype(bf)
    block_out = residual + lax.psum_scatter(
        mixture, "tensor", scatter_dimension=0, tiled=True
    ).astype(f32)
    grad_down = lax.psum_scatter(down_local, "dp", scatter_dimension=0, tiled=True)
    grad_down = grad_down.astype(f32).reshape(rows, experts, units).transpose(1, 0, 2)
    grad_gate_up = lax.psum_scatter(gate_up_local, "dp", scatter_dimension=0, tiled=True)
    grad_gate_up = grad_gate_up.astype(f32).reshape(rows, 2, experts, units).transpose(2, 1, 0, 3)
    scaled_two = gain_two * normed_two_cot
    residual_cot = (
        cotangent
        + inv_two * scaled_two
        - residual * inv_two**3 * jnp.mean(scaled_two * residual, axis=1, keepdims=True)
    )
    resid_all = lax.all_gather(residual_cot.astype(bf), "tensor", axis=0, tiled=True)
    out_local = lax.dot_general(
        resid_all, attended_flat, (((0,), (0,)), ((), ())), preferred_element_type=f32
    )
    attended_cot = jnp.dot(resid_all, out_all, preferred_element_type=f32).astype(bf)
    attended_cot = attended_cot.reshape(seq_count, SEQ, 2, kv_count, HEAD_SIZE).transpose(
        0, 2, 1, 3, 4
    )
    query_cot, key_cot, value_cot = lax.map(
        attend_back, (queries, keys_rot, values, attended, log_totals, attended_cot)
    )
    query_plain = unrotate(query_cot, cos_table, sine_table)
    key_plain = unrotate(key_cot, cos_table, sine_table)
    proj_cot = jnp.concatenate(
        [
            query_plain[:, 0].reshape(tok_count, cols),
            query_plain[:, 1].reshape(tok_count, cols),
            key_plain.reshape(tok_count, cols),
            value_cot.reshape(tok_count, cols),
        ],
        axis=1,
    ).astype(bf)
    attn_local = lax.dot_general(
        tokens_one, proj_cot, (((0,), (0,)), ((), ())), preferred_element_type=f32
    )
    norm_terms = lax.dot_general(
        proj_cot, proj_all, (((1,), (1,)), ((), ())), preferred_element_type=f32
    )
    normed_one_cot = lax.psum_scatter(
        norm_terms.astype(bf), "tensor", scatter_dimension=0, tiled=True
    ).astype(f32)
    both_local = jnp.concatenate([attn_local, out_local], axis=1).astype(bf)
    both_sum = lax.psum_scatter(both_local, "dp", scatter_dimension=0, tiled=True).astype(f32)
    both_sum = both_sum.reshape(rows, 6, cols).transpose(1, 0, 2)
    grad_attn = both_sum[:4]
    grad_out = both_sum[4:]
    scaled_one = gain_one * normed_one_cot
    input_grad = (
        residual_cot
        + inv_one * scaled_one
        - block_in * inv_one**3 * jnp.mean(scaled_one * block_in, axis=1, keepdims=True)
    )
    gain_local = jnp.stack(
        [
            jnp.sum(normed_one_cot * block_in * inv_one, axis=0),
            jnp.sum(normed_two_cot * residual * inv_two, axis=0),
        ]
    )
    gain_sum = lax.psum(gain_local, ("dp", "tensor"))
    grad_gains = lax.dynamic_slice_in_dim(gain_sum, lax.axis_index("dp") * rows, rows, axis=1)
    new_gains, new_m_gains, new_v_gains = adamw_update(
        norm_gains, m_gains, v_gains, grad_gains, rate_gain, 0.0
    )
    new_attn, new_m_attn, new_v_attn = adamw_update(
        attention_weight,
        attention_first_moment,
        attention_second_moment,
        grad_attn,
        rate_matrix,
        decay_matrix,
    )
    new_out, new_m_out, new_v_out = adamw_update(
        output_weight,
        output_first_moment,
        output_second_moment,
        grad_out,
        rate_matrix,
        decay_matrix,
    )
    new_gate_up, new_m_gate_up, new_v_gate_up = adamw_update(
        w_gate_up, m_gate_up, v_gate_up, grad_gate_up, rate_matrix, decay_matrix
    )
    new_down, new_m_down, new_v_down = adamw_update(
        w_down, m_down, v_down, grad_down, rate_matrix, decay_matrix
    )
    return (
        block_out,
        input_grad,
        grad_gains,
        grad_attn,
        grad_out,
        grad_gate_up,
        grad_down,
        new_gains,
        new_attn,
        new_out,
        new_gate_up,
        new_down,
        new_m_gains,
        new_v_gains,
        new_m_attn,
        new_v_attn,
        new_m_out,
        new_v_out,
        new_m_gate_up,
        new_v_gate_up,
        new_m_down,
        new_v_down,
    )


def solution(mesh):
    return jax.shard_map(
        local,
        mesh=mesh,
        in_specs=(
            P(("dp", "tensor"), None),
            P(("dp", "tensor"), None),
            P("dp", None),
            P("dp", None),
            P(None, "dp"),
            P(None, "dp", "tensor"),
            P(None, "dp", "tensor"),
            P(None, None, "dp", "tensor"),
            P(None, "dp", "tensor"),
            P(None, "dp"),
            P(None, "dp"),
            P(None, "dp", "tensor"),
            P(None, "dp", "tensor"),
            P(None, "dp", "tensor"),
            P(None, "dp", "tensor"),
            P(None, None, "dp", "tensor"),
            P(None, None, "dp", "tensor"),
            P(None, "dp", "tensor"),
            P(None, "dp", "tensor"),
        ),
        out_specs=(
            P(("dp", "tensor"), None),
            P(("dp", "tensor"), None),
            P(None, "dp"),
            P(None, "dp", "tensor"),
            P(None, "dp", "tensor"),
            P(None, None, "dp", "tensor"),
            P(None, "dp", "tensor"),
            P(None, "dp"),
            P(None, "dp", "tensor"),
            P(None, "dp", "tensor"),
            P(None, None, "dp", "tensor"),
            P(None, "dp", "tensor"),
            P(None, "dp"),
            P(None, "dp"),
            P(None, "dp", "tensor"),
            P(None, "dp", "tensor"),
            P(None, "dp", "tensor"),
            P(None, "dp", "tensor"),
            P(None, None, "dp", "tensor"),
            P(None, None, "dp", "tensor"),
            P(None, "dp", "tensor"),
            P(None, "dp", "tensor"),
        ),
        check_vma=False,
    )
```

profile of v0, /device:TPU:0, one launch (start us, length us, event | category | flops | bytes accessed | tf_op | source)
XLA Modules:
  0.0 598.8 jit_solution(3122732607899009950)
XLA Ops:
  7.9 10.3 %all_gather.24 = bf16[2,1024]{1,0:T(2,128)(2,1)S(1)} all-gather(bf16[2,128]{1,0:T(2,128)(2,1)S(1)} %convert_element_type.108), channel_id=1, replica_groups=mesh['dp'=8,'tensor'=4] {'dp'}, dimensions={1}, use_global_device_ids=true | all-gather | bytes 4608 | tf_op jit(solution)/shard_map/all_gather | solution.py:143
  18.2 1.2 multiply_reduce_fusion.2
  19.9 1.9 multiply_convert_fusion.3
  21.8 1.1 copy.84
  25.1 25.1 %all-gather.8.cloned.1.call-done = bf16[512,1024]{1,0:T(8,128)(2,1)} async-done(((bf16[128,1024]{1,0:T(8,128)(2,1)}), bf16[512,1024]{1,0:T(8,128)(2,1)}) %all-gather.8.cloned.1.call-update) | async-done | bytes 1048592 | tf_op jit(solution)/shard_map/all_gather | solution.py:156
  50.2 27.6 %all-gather.10.cloned.1.call-done = bf16[1024,768]{0,1:T(8,128)(2,1)} async-done(((bf16[128,768]{0,1:T(8,128)(2,1)}), bf16[1024,768]{0,1:T(8,128)(2,1)}) %all-gather.10.cloned.1.call-update) | async-done | bytes 1572880 | tf_op jit(solution)/shard_map/all_gather | solution.py:146
  77.8 2.3 fusion.21
  84.6 2.5 convolution_convert_fusion.1
  87.2 27.4 %reduce-scatter.12.cloned.1.call-done = bf16[128,1024]{1,0:T(8,128)(2,1)} async-done(((bf16[512,1024]{1,0:T(8,128)(2,1)}), bf16[128,1024]{1,0:T(8,128)(2,1)}) %reduce-scatter.12.cloned.1.call-update) | async-done | bytes 262160 | tf_op jit(solution)/shard_map/reduce_scatter | solution.py:168
  114.6 1.1 multiply_reduce_fusion.1
  117.6 2.6 copy.89
  120.2 1.8 convert_element_type.122
  122.1 2.3 copy.91
  124.9 1.4 select_reduce_fusion
  126.3 1.6 copy.90
  127.9 16.3 %all-gather.12.cloned.1.call-done = bf16[512,1024]{1,0:T(8,128)(2,1)} async-done(((bf16[128,1024]{1,0:T(8,128)(2,1)}), bf16[512,1024]{1,0:T(8,128)(2,1)}) %all-gather.12.cloned.1.call-update) | async-done | bytes 1048592 | tf_op jit(solution)/shard_map/all_gather | solution.py:173
  144.2 57.6 %all-gather.14.cloned.1.call-done = bf16[1024,4096]{0,1:T(8,128)(2,1)} async-done(((bf16[128,4096]{0,1:T(8,128)(2,1)}), bf16[1024,4096]{0,1:T(8,128)(2,1)}) %all-gather.14.cloned.1.call-update) | async-done | bytes 8388624 | tf_op jit(solution)/shard_map/all_gather | solution.py:157
  201.8 11.5 %fusion.68 = f32[512,4096]{1,0:T(8,128)} fusion(bf16[512,1024]{1,0:T(8,128)(2,1)} %all-gather.12.cloned.1.call-done, bf16[1024,4096]{0,1:T(8,128)(2,1)} %all-gather.14.cloned.1.call-done), kind=kOutput, calls=%fused_computation.141 | convolution fusion | flops 4294967296 | bytes 17825792 | tf_op jit(solution)/shard_map/dot_general | solution.py:182
  213.3 18.5 %all-gather.18.cloned.1.call-done = bf16[512,1024]{1,0:T(8,128)(2,1)} async-done(((bf16[128,1024]{1,0:T(8,128)(2,1)}), bf16[512,1024]{1,0:T(8,128)(2,1)}) %all-gather.18.cloned.1.call-update) | async-done | bytes 1048592 | tf_op jit(solution)/shard_map/all_gather | solution.py:159
  231.8 39.2 %all-gather.16.cloned.1.call-done = bf16[1024,2048]{0,1:T(8,128)(2,1)} async-done(((bf16[128,2048]{0,1:T(8,128)(2,1)}), bf16[1024,2048]{0,1:T(8,128)(2,1)}) %all-gather.16.cloned.1.call-update) | async-done | bytes 4194320 | tf_op jit(solution)/shard_map/all_gather | solution.py:158
  271.0 2.2 broadcast_in_dim.81
  273.2 10.1 %multiply_convert_fusion.1 = (bf16[512,2048]{1,0:T(8,128)(2,1)S(1)}, bf16[512,2048]{1,0:T(8,128)(2,1)S(1)}, bf16[512,2048]{1,0:T(8,128)(2,1)}) fusion(f32[512,4096]{1,0:T(8,128)} %fusion.68, f32[64,8,16,128]{3,2,1,0:T(8,128)S(1)} %bitcast.152, bf16[512,1024]{1,0:T(8,128)(2,1)} %all-gather.18.cloned.1.call-done, ...), kind=kOutput, calls=%fused_computation.11 | convolution fusion | flops 2166358016 | bytes 24117248 | tf_op jit(solution)/shard_map/dot_general | solution.py:187
  283.3 1.3 copy-done.39
  285.4 5.5 fusion.9
  291.1 6.1 %convolution_convert_fusion.4 = bf16[512,1024]{1,0:T(8,128)(2,1)} fusion(bf16[512,2048]{1,0:T(8,128)(2,1)} %get-tuple-element.99, bf16[1024,2048]{0,1:T(8,128)(2,1)} %all-gather.16.cloned.1.call-done), kind=kOutput, calls=%fused_computation.32 | convolution fusion | flops 2148007936 | bytes 7340032 | tf_op jit(solution)/shard_map/dot_general | solution.py:205
  297.3 21.0 %reduce-scatter.16.cloned.1.call-done = bf16[128,1024]{1,0:T(8,128)(2,1)} async-done(((bf16[512,1024]{1,0:T(8,128)(2,1)}), bf16[128,1024]{1,0:T(8,128)(2,1)}) %reduce-scatter.16.cloned.1.call-update) | async-done | bytes 262160 | tf_op jit(solution)/shard_map/reduce_scatter | solution.py:196
  318.3 1.7 fusion.34
  320.5 26.5 %reduce-scatter.14.cloned.1.call-done = bf16[128,1024]{1,0:T(8,128)(2,1)} async-done(((bf16[512,1024]{1,0:T(8,128)(2,1)}), bf16[128,1024]{1,0:T(8,128)(2,1)}) %reduce-scatter.14.cloned.1.call-update) | async-done | bytes 262160 | tf_op jit(solution)/shard_map/reduce_scatter | solution.py:208
  347.0 2.5 fusion.65
  349.6 26.6 %all-gather.20.cloned.1.call-done = bf16[512,1024]{1,0:T(8,128)(2,1)} async-done(((bf16[128,1024]{1,0:T(8,128)(2,1)}), bf16[512,1024]{1,0:T(8,128)(2,1)}) %all-gather.20.cloned.1.call-update) | async-done | bytes 1048592 | tf_op jit(solution)/shard_map/all_gather | solution.py:221
  376.1 1.8 bitcast_convert_fusion
  379.1 3.8 fusion.2
  385.5 1.7 convolution_convert_fusion.3
  387.8 2.0 convolution_convert_fusion.2
  389.9 1.6 copy.113
  391.6 6.1 %convert_bitcast_fusion = bf16[1024,2048]{0,1:T(8,128)(2,1)} fusion(bf16[512,2048]{1,0:T(8,128)(2,1)} %get-tuple-element.99, bf16[512,1024]{1,0:T(8,128)(2,1)S(1)} %copy-done.37), kind=kOutput, calls=%fused_computation.9 | convolution fusion | flops 2149580800 | bytes 7340032 | tf_op jit(solution)/shard_map/dot_general | solution.py:199
  397.7 6.5 %copy.115 = bf16[1024,2048]{1,0:T(8,128)(2,1)} copy(bf16[1024,2048]{0,1:T(8,128)(2,1)} %convert_bitcast_fusion) | data formatting | bytes 8388608
  405.5 9.0 %convolution_convert_fusion = bf16[1024,4096]{1,0:T(8,128)(2,1)} fusion(bf16[512,1024]{1,0:T(8,128)(2,1)S(1)} %copy-done.36, bf16[512,2048]{1,0:T(8,128)(2,1)} %copy-done.40, bf16[512,2048]{1,0:T(8,128)(2,1)} %copy-done.39), kind=kOutput, calls=%fused_computation | convolution fusion | flops 4307550208 | bytes 13631488 | tf_op jit(solution)/shard_map/dot_general | solution.py:202
  415.2 1.1 fusion.36
  416.3 40.0 %psum.7 = f32[2,1024]{1,0:T(2,128)S(1)} all-reduce(f32[2,1024]{1,0:T(2,128)S(1)} %pad_maximum_fusion.14), channel_id=1, replica_groups=mesh['dp'=8,'tensor'=4] {'dp','tensor'}, use_global_device_ids=true, to_apply=%region_13.14 | all-reduce | flops 2048 | bytes 16384 | tf_op jit(solution)/shard_map/psum | solution.py:269
  457.0 1.9 fusion.28
  458.9 1.1 copy.114
  462.0 47.7 %reduce-scatter.24.cloned.1.call-done = bf16[128,2048]{1,0:T(8,128)(2,1)} async-done(((bf16[1024,2048]{1,0:T(8,128)(2,1)}), bf16[128,2048]{1,0:T(8,128)(2,1)}) %reduce-scatter.24.cloned.1.call-update) | async-done | bytes 524304
  509.8 1.3 copy.116
  512.3 3.7 multiply_subtract_fusion.1
  516.0 68.6 %reduce-scatter.20.cloned.1.call-done = bf16[128,4096]{1,0:T(8,128)(2,1)} async-done(((bf16[1024,4096]{1,0:T(8,128)(2,1)}), bf16[128,4096]{1,0:T(8,128)(2,1)}) %reduce-scatter.20.cloned.1.call-update) | async-done | bytes 1048592 | tf_op jit(solution)/shard_map/reduce_scatter | solution.py:213
  584.6 1.6 convert_bitcast_fusion.1
  587.1 4.9 multiply_subtract_fusion
  (157 shorter events, 22.8 us)
Async XLA Ops:
  7.2 43.0 %all-gather.8.cloned.1.call-start = ((), (), s32[]{:S(2)}) async-start(), calls=%async_computation.7 | async-start | bytes 1310720 | tf_op jit(solution)/shard_map/all_gather | solution.py:156
  19.9 1.9 copy-start.30
  21.8 56.1 %all-gather.10.cloned.1.call-start = ((), (), s32[]{:S(2)}) async-start(), calls=%async_computation.8 | async-start | bytes 1769472 | tf_op jit(solution)/shard_map/all_gather | solution.py:146
  24.6 89.9 %reduce-scatter.12.cloned.1.call-start = ((), (), s32[]{:S(2)}) async-start(), calls=%async_computation.9 | async-start | bytes 1310720 | tf_op jit(solution)/shard_map/reduce_scatter | solution.py:168
  24.8 58.2 %copy-start.7 = (pred[512,512]{0,1:T(8,128)(4,1)}, pred[512,512]{0,1:T(8,128)(4,1)S(1)}, u32[]{:S(2)}) copy-start(pred[512,512]{0,1:T(8,128)(4,1)S(1)} %iota_compare_fusion) | copy-start | bytes 786436
  80.2 3.7 copy-start.4
  80.4 1.7 copy-start.17
  80.4 1.7 copy-start.22
  82.1 2.0 copy-start
  84.0 30.5 %copy-start.1 = (f32[128,1024]{1,0:T(8,128)S(1)}, f32[128,1024]{1,0:T(8,128)}, u32[]{:S(2)}) copy-start(f32[128,1024]{1,0:T(8,128)} %param.19) | copy-start | bytes 1572868
  84.5 2.7 copy-start.9
  87.1 57.1 %all-gather.12.cloned.1.call-start = ((), (), s32[]{:S(2)}) async-start(), calls=%async_computation.10 | async-start | bytes 1310720 | tf_op jit(solution)/shard_map/all_gather | solution.py:173
  117.6 84.2 %all-gather.14.cloned.1.call-start = ((), (), s32[]{:S(2)}) async-start(), calls=%async_computation.11 | async-start | bytes 9437184 | tf_op jit(solution)/shard_map/all_gather | solution.py:157
  120.2 111.6 %all-gather.18.cloned.1.call-start = ((), (), s32[]{:S(2)}) async-start(), calls=%async_computation.14 | async-start | bytes 1310720 | tf_op jit(solution)/shard_map/all_gather | solution.py:159
  122.0 148.9 %all-gather.16.cloned.1.call-start = ((), (), s32[]{:S(2)}) async-start(), calls=%async_computation.12 | async-start | bytes 4718592 | tf_op jit(solution)/shard_map/all_gather | solution.py:158
  124.4 193.9 %reduce-scatter.16.cloned.1.call-start = ((), (), s32[]{:S(2)}) async-start(), calls=%async_computation.15 | async-start | bytes 1310720 | tf_op jit(solution)/shard_map/reduce_scatter | solution.py:196
  271.0 14.4 %slice-start = ((s8[8388608]{0:T(1024)(128)(4,1)}), s8[4194304]{0:T(1024)(128)(4,1)S(1)}, s32[]{:S(2)}) async-start(s8[8388608]{0:T(1024)(128)(4,1)} %bitcast.179), calls=%async_computation.21 | async-start | bytes 8388608
  273.2 12.1 %slice-start.1 = ((s8[8388608]{0:T(1024)(128)(4,1)}), s8[4194304]{0:T(1024)(128)(4,1)S(1)}, s32[]{:S(2)}) async-start(s8[8388608]{0:T(1024)(128)(4,1)} %bitcast.179), calls=%async_computation.22 | async-start | bytes 8388608
  283.3 2.0 copy-start.40
  290.8 56.2 %reduce-scatter.14.cloned.1.call-start = ((), (), s32[]{:S(2)}) async-start(), calls=%async_computation.13 | async-start | bytes 1310720 | tf_op jit(solution)/shard_map/reduce_scatter | solution.py:208
  297.2 78.9 %all-gather.20.cloned.1.call-start = ((), (), s32[]{:S(2)}) async-start(), calls=%async_computation.16 | async-start | bytes 1310720 | tf_op jit(solution)/shard_map/all_gather | solution.py:221
  349.5 29.5 %copy-start.8 = (pred[512,512]{0,1:T(8,128)(4,1)S(1)}, pred[512,512]{0,1:T(8,128)(4,1)}, u32[]{:S(2)}) copy-start(pred[512,512]{0,1:T(8,128)(4,1)} %copy-done.7) | copy-start | bytes 786436
  349.5 65.2 %reduce-scatter.18.cloned.1.call-start = ((), (), s32[]{:S(2)}) async-start(), calls=%async_computation.17 | async-start | bytes 1310720 | tf_op jit(solution)/shard_map/reduce_scatter | solution.py:249
  379.0 3.8 copy-start.21
  379.0 3.8 copy-start.23
  379.0 4.3 copy-start.16
  379.1 4.3 copy-start.18
  385.1 2.3 copy-start.6
  387.3 71.6 %reduce-scatter.22.cloned.1.call-start = ((), (), s32[]{:S(2)}) async-start(), calls=%async_computation.19 | async-start | bytes 1769472
  389.9 1.7 copy-start.37
  391.5 118.2 %reduce-scatter.24.cloned.1.call-start = ((), (), s32[]{:S(2)}) async-start(), calls=%async_computation.20 | async-start | bytes 4718592
  404.3 180.4 %reduce-scatter.20.cloned.1.call-start = ((), (), s32[]{:S(2)}) async-start(), calls=%async_computation.18 | async-start | bytes 9437184 | tf_op jit(solution)/shard_map/reduce_scatter | solution.py:213
  414.5 1.8 copy-start.28
  414.5 41.9 %copy-start.32 = (f32[2,128]{1,0:T(2,128)S(1)}, f32[2,128]{1,0:T(2,128)}, u32[]{:S(2)}) copy-start(f32[2,128]{1,0:T(2,128)} %param.23) | copy-start | bytes 3076
  414.5 41.9 %copy-start.33 = (f32[2,128]{1,0:T(2,128)S(1)}, f32[2,128]{1,0:T(2,128)}, u32[]{:S(2)}) copy-start(f32[2,128]{1,0:T(2,128)} %param.28) | copy-start | bytes 3076
  414.5 41.8 %copy-start.34 = (f32[2,128]{1,0:T(2,128)S(1)}, f32[2,128]{1,0:T(2,128)}, u32[]{:S(2)}) copy-start(f32[2,128]{1,0:T(2,128)} %param.29) | copy-start | bytes 3076
  414.5 42.4 %copy-start.10 = (f32[128,1024]{1,0:T(8,128)S(1)}, f32[128,1024]{1,0:T(8,128)}, u32[]{:S(2)}) copy-start(f32[128,1024]{1,0:T(8,128)} %get-tuple-element.94) | copy-start | bytes 1572868
  414.5 42.4 %copy-start.35 = (f32[128]{0:T(128)S(1)}, f32[128]{0:T(128)}, u32[]{:S(2)}) copy-start(f32[128]{0:T(128)} %get-tuple-element.113) | copy-start | bytes 1540
  414.6 45.6 %copy-start.19 = (f32[2,128,128]{2,1,0:T(8,128)S(1)}, f32[2,128,128]{2,1,0:T(8,128)}, u32[]{:S(2)}) copy-start(f32[2,128,128]{2,1,0:T(8,128)} %param.25) | copy-start | bytes 393220
  414.6 45.6 %copy-start.26 = (f32[2,128,128]{2,1,0:T(8,128)S(1)}, f32[2,128,128]{2,1,0:T(8,128)}, u32[]{:S(2)}) copy-start(f32[2,128,128]{2,1,0:T(8,128)} %param.32) | copy-start | bytes 393220
  414.6 45.6 %copy-start.27 = (f32[2,128,128]{2,1,0:T(8,128)S(1)}, f32[2,128,128]{2,1,0:T(8,128)}, u32[]{:S(2)}) copy-start(f32[2,128,128]{2,1,0:T(8,128)} %param.33) | copy-start | bytes 393220
  414.6 46.4 %copy-start.13 = (f32[4,128,128]{2,1,0:T(8,128)S(1)}, f32[4,128,128]{2,1,0:T(8,128)}, u32[]{:S(2)}) copy-start(f32[4,128,128]{2,1,0:T(8,128)} %param.24) | copy-start | bytes 786436
  414.6 46.4 %copy-start.24 = (f32[4,128,128]{2,1,0:T(8,128)S(1)}, f32[4,128,128]{2,1,0:T(8,128)}, u32[]{:S(2)}) copy-start(f32[4,128,128]{2,1,0:T(8,128)} %param.30) | copy-start | bytes 786436
  414.6 46.4 %copy-start.25 = (f32[4,128,128]{2,1,0:T(8,128)S(1)}, f32[4,128,128]{2,1,0:T(8,128)}, u32[]{:S(2)}) copy-start(f32[4,128,128]{2,1,0:T(8,128)} %param.31) | copy-start | bytes 786436
  460.0 52.3 %copy-start.3 = (f32[16,128,128]{2,1,0:T(8,128)S(1)}, f32[16,128,128]{2,1,0:T(8,128)}, u32[]{:S(2)}) copy-start(f32[16,128,128]{2,1,0:T(8,128)} %param.27) | copy-start | bytes 3145732
  516.0 70.5 %copy-start.2 = (f32[16,2,128,128]{3,2,1,0:T(8,128)S(1)}, f32[16,2,128,128]{3,2,1,0:T(8,128)}, u32[]{:S(2)}) copy-start(f32[16,2,128,128]{3,2,1,0:T(8,128)} %param.26) | copy-start | bytes 6291460
  584.6 2.0 copy-start.11
  584.6 2.5 copy-start.12
  (9 other events, 9.2 us)
Sparse Core Ops, SparseCore 0:
  21.9 28.2 all-gather.7
  52.6 25.1 all-gather.9
  87.3 27.2 reduce-scatter.11
  117.7 26.4 all-gather.11
  146.5 55.2 all-gather.13
  203.8 27.9 all-gather.17
  234.2 36.7 all-gather.15
  291.0 27.2 reduce-scatter.15
  321.2 25.7 reduce-scatter.13
  349.6 26.4 all-gather.19
  387.4 26.6 reduce-scatter.17
  417.8 37.1 reduce-scatter.21
  458.3 51.3 reduce-scatter.23
  513.1 71.4 reduce-scatter.19
where the time goes:
time: 605 us; the launch traced here: 599 us
  waiting for transfers between devices  402 us (66%)
  matrix products  66.3 us (11%)
  blocking collectives  50.3 us (8%)
  other arithmetic  34.6 us (6%)
  local copies, waits for them, and re-layouts  29 us (5%)
  between operations  14.9 us (2%)
    reduce_scatter x1, waiting for transfers between devices, local(): lax.psum_scatter(gate_up_local, 'dp', scatter_dimension=0, tiled=True)  68.6 us
    all_gather x1, waiting for transfers between devices, local(): gate_up_all = lax.all_gather(gate_up_rows, 'dp', axis=0, tiled=True)  57.6 us
    unnamed x16, waiting for transfers between devices  48 us
    psum x1, blocking collectives, local(): gain_sum = lax.psum(gain_local, ('dp', 'tensor'))  40 us
    all_gather x1, waiting for transfers between devices, local(): down_all = lax.all_gather(down_rows, 'dp', axis=0, tiled=True)  39.2 us
    all_gather x1, waiting for transfers between devices, local(): attn_all = lax.all_gather(attn_rows, 'dp', axis=0, tiled=True)  27.6 us
    reduce_scatter x1, waiting for transfers between devices, local(): lax.psum_scatter(partial_value, 'tensor', scatter_dimension=0, tiled=True)  27.4 us
    all_gather x1, waiting for transfers between devices, local(): lax.all_gather(residual_cot.astype(bf), 'tensor', axis=0, tiled=True)  26.6 us
  transfers between devices with their start and end apart: 14, of which 12 were waited for; matrix products, arithmetic and copies ran while one was open for 12% of the time, Pallas kernels for 0%

commit v1 on v0

--- a/solution.py
+++ b/solution.py
@@ -155,7 +155,14 @@
     normed_one = (block_in * inv_one * gain_one).astype(bf)
     tokens_one = lax.all_gather(normed_one, "tensor", axis=0, tiled=True)
     gate_up_all = lax.all_gather(gate_up_rows, "dp", axis=0, tiled=True)
-    down_all = lax.all_gather(down_rows, "dp", axis=0, tiled=True)
+    ways = lax.axis_size("dp")
+    pieces = [down_rows]
+    for far in range(1, ways):
+        pieces.append(
+            lax.ppermute(pieces[far - 1], "dp", [(d, (d - 1) % ways) for d in range(ways)])
+        )
+    line = jnp.concatenate(pieces, axis=0)
+    down_all = jnp.roll(line, lax.axis_index("dp") * down_rows.shape[0], axis=0)
     cot_all = lax.all_gather(cotangent.astype(bf), "tensor", axis=0, tiled=True)
     projected = jnp.dot(tokens_one, proj_all, preferred_element_type=f32)
     head_vals = projected.reshape(seq_count, SEQ, 4, kv_count, HEAD_SIZE).transpose(2, 0, 1, 3, 4)

time: 605 us -> 579 us (0.957)
  waiting for transfers between devices: 402 us -> 331 us
  local copies, waits for them, and re-layouts: 29 us -> 53.7 us
  starting transfers between devices: 1.43 us -> 20.4 us
    all_gather x1, waiting for transfers between devices: 57.6 us -> 0.01 us  [local(): gate_up_all = lax.all_gather(gate_up_rows, 'dp', axis=0, tiled=True)]
    ppermute x0 -> x7, waiting for transfers between devices: none -> 54.3 us  [local(): lax.ppermute(pieces[far - 1], 'dp', [(d, (d - 1) % ways) for d in range(w...]
    all_gather x1 -> x0, waiting for transfers between devices: 39.2 us -> none  [local(): down_all = lax.all_gather(down_rows, 'dp', axis=0, tiled=True)]
    unnamed x95 -> x118, local copies, waits for them, and re-layouts: 24.7 us -> 48.5 us
    ppermute x0 -> x7, starting transfers between devices: none -> 19.5 us  [local(): lax.ppermute(pieces[far - 1], 'dp', [(d, (d - 1) % ways) for d in range(w...]
    all_gather x1, waiting for transfers between devices: 16.3 us -> 0.01 us  [local(): tokens_two = lax.all_gather(normed_two, 'tensor', axis=0, tiled=True)]
    all_gather x1, waiting for transfers between devices: 18.5 us -> 6.51 us  [local(): cot_all = lax.all_gather(cotangent.astype(bf), 'tensor', axis=0, tiled=True)]
    unnamed x16 -> x15, waiting for transfers between devices: 48 us -> 47.6 us
  transfers between devices with their start and end apart: 14 -> 20, of which waited for: 12 -> 16; matrix products, arithmetic and copies ran while one was open for 12% -> 16% of each run, Pallas kernels for 0% -> 0%
where the time goes in v1:
time: 579 us; the launch traced here: 572 us
  waiting for transfers between devices  331 us (57%)
  matrix products  66.5 us (11%)
  local copies, waits for them, and re-layouts  53.7 us (9%)
  blocking collectives  50.4 us (9%)
  other arithmetic  35.1 us (6%)
  starting transfers between devices  20.4 us (4%)
  between operations  14.8 us (3%)
    reduce_scatter x1, waiting for transfers between devices, local(): lax.psum_scatter(gate_up_local, 'dp', scatter_dimension=0, tiled=True)  69.2 us
    ppermute x7, waiting for transfers between devices, local(): lax.ppermute(pieces[far - 1], 'dp', [(d, (d - 1) % ways) for d in range(w...  54.3 us
    unnamed x118, local copies, waits for them, and re-layouts  48.5 us
    unnamed x15, waiting for transfers between devices  47.6 us
    psum x1, blocking collectives, local(): gain_sum = lax.psum(gain_local, ('dp', 'tensor'))  40.1 us
    all_gather x1, waiting for transfers between devices, local(): attn_all = lax.all_gather(attn_rows, 'dp', axis=0, tiled=True)  27.6 us
    reduce_scatter x1, waiting for transfers between devices, local(): lax.psum_scatter(partial_value, 'tensor', scatter_dimension=0, tiled=True)  27.4 us
    all_gather x1, waiting for transfers between devices, local(): lax.all_gather(residual_cot.astype(bf), 'tensor', axis=0, tiled=True)  26.6 us
  transfers between devices with their start and end apart: 20, of which 16 were waited for; matrix products, arithmetic and copies ran while one was open for 16% of the time, Pallas kernels for 0%

profile of v1, /device:TPU:0, one launch (start us, length us, event | category | flops | bytes accessed | tf_op | source)
XLA Modules:
  0.0 572.2 jit_solution(1628435520069264801)
XLA Ops:
  7.9 10.3 %all_gather.21 = bf16[2,1024]{1,0:T(2,128)(2,1)S(1)} all-gather(bf16[2,128]{1,0:T(2,128)(2,1)S(1)} %convert_element_type.108), channel_id=1, replica_groups=mesh['dp'=8,'tensor'=4] {'dp'}, dimensions={1}, use_global_device_ids=true | all-gather | bytes 4608 | tf_op jit(solution)/shard_map/all_gather | solution.py:143
  25.1 25.1 %all-gather.7.cloned.1.call-done = bf16[512,1024]{1,0:T(8,128)(2,1)} async-done(((bf16[128,1024]{1,0:T(8,128)(2,1)}), bf16[512,1024]{1,0:T(8,128)(2,1)}) %all-gather.7.cloned.1.call-update) | async-done | bytes 1048592 | tf_op jit(solution)/shard_map/all_gather | solution.py:156
  50.2 27.6 %all-gather.9.cloned.1.call-done = bf16[1024,768]{0,1:T(8,128)(2,1)} async-done(((bf16[128,768]{0,1:T(8,128)(2,1)}), bf16[1024,768]{0,1:T(8,128)(2,1)}) %all-gather.9.cloned.1.call-update) | async-done | bytes 1572880 | tf_op jit(solution)/shard_map/all_gather | solution.py:146
  77.8 2.3 fusion.30
  84.5 2.5 convolution_convert_fusion.1
  87.1 27.4 %reduce-scatter.12.cloned.1.call-done = bf16[128,1024]{1,0:T(8,128)(2,1)} async-done(((bf16[512,1024]{1,0:T(8,128)(2,1)}), bf16[128,1024]{1,0:T(8,128)(2,1)}) %reduce-scatter.12.cloned.1.call-update) | async-done | bytes 262160 | tf_op jit(solution)/shard_map/reduce_scatter | solution.py:175
  117.5 2.6 copy.92
  120.1 2.2 copy.94
  123.8 7.0 %collective-permute-done = bf16[128,2048]{0,1:T(8,128)(2,1)S(1)} collective-permute-done((bf16[128,2048]{0,1:T(8,128)(2,1)}, bf16[128,2048]{0,1:T(8,128)(2,1)S(1)}, u32[]{:S(2)}, u32[]{:S(2)}) %collective-permute-start) | collective-permute-done | bytes 524320 | tf_op jit(solution)/shard_map/ppermute | solution.py:162
  131.6 3.1 collective-permute-start.1
  134.7 6.7 %collective-permute-done.1 = bf16[128,2048]{0,1:T(8,128)(2,1)S(1)} collective-permute-done((bf16[128,2048]{0,1:T(8,128)(2,1)S(1)}, bf16[128,2048]{0,1:T(8,128)(2,1)S(1)}, u32[]{:S(2)}, u32[]{:S(2)}) %collective-permute-start.1) | collective-permute-done | bytes 524320 | tf_op jit(solution)/shard_map/ppermute | solution.py:162
  142.2 3.2 collective-permute-start.2
  145.4 6.7 %collective-permute-done.2 = bf16[128,2048]{0,1:T(8,128)(2,1)S(1)} collective-permute-done((bf16[128,2048]{0,1:T(8,128)(2,1)S(1)}, bf16[128,2048]{0,1:T(8,128)(2,1)S(1)}, u32[]{:S(2)}, u32[]{:S(2)}) %collective-permute-start.2) | collective-permute-done | bytes 524320 | tf_op jit(solution)/shard_map/ppermute | solution.py:162
  152.9 2.8 collective-permute-start.3
  155.7 15.3 %collective-permute-done.3 = bf16[128,2048]{0,1:T(8,128)(2,1)} collective-permute-done((bf16[128,2048]{0,1:T(8,128)(2,1)S(1)}, bf16[128,2048]{0,1:T(8,128)(2,1)}, u32[]{:S(2)}, u32[]{:S(2)}) %collective-permute-start.3) | collective-permute-done | bytes 524320 | tf_op jit(solution)/shard_map/ppermute | solution.py:162
  171.0 3.0 collective-permute-start.4
  178.8 2.1 constant_dynamic-update-slice_fusion.15
  180.9 4.3 collective-permute-done.4
  185.3 2.8 collective-permute-start.5
  188.1 2.0 constant_dynamic-update-slice_fusion.14
  190.0 2.0 constant_dynamic-update-slice_fusion.13
  192.1 2.0 constant_dynamic-update-slice_fusion.12
  194.1 12.4 %collective-permute-done.5 = bf16[128,2048]{0,1:T(8,128)(2,1)S(1)} collective-permute-done((bf16[128,2048]{0,1:T(8,128)(2,1)}, bf16[128,2048]{0,1:T(8,128)(2,1)S(1)}, u32[]{:S(2)}, u32[]{:S(2)}) %collective-permute-start.5) | collective-permute-done | bytes 524320 | tf_op jit(solution)/shard_map/ppermute | solution.py:162
  206.4 3.2 collective-permute-start.6
  211.6 1.9 constant_dynamic-update-slice_fusion.10
  214.4 1.9 collective-permute-done.6
  220.8 2.0 constant_dynamic-update-slice_fusion.3
  226.6 11.6 %fusion.79 = f32[512,4096]{1,0:T(8,128)} fusion(bf16[512,1024]{1,0:T(8,128)(2,1)} %all-gather.11.cloned.1.call-done, bf16[1024,4096]{0,1:T(8,128)(2,1)} %all-gather.13.cloned.1.call-done), kind=kOutput, calls=%fused_computation.163 | convolution fusion | flops 4294967296 | bytes 17825792 | tf_op jit(solution)/shard_map/dot_general | solution.py:189
  238.2 6.5 %all-gather.15.cloned.1.call-done = bf16[512,1024]{1,0:T(8,128)(2,1)} async-done(((bf16[128,1024]{1,0:T(8,128)(2,1)}), bf16[512,1024]{1,0:T(8,128)(2,1)}) %all-gather.15.cloned.1.call-update) | async-done | bytes 1048592 | tf_op jit(solution)/shard_map/all_gather | solution.py:166
  244.7 2.2 broadcast_in_dim.81
  246.9 10.1 %multiply_convert_fusion.1 = (bf16[512,2048]{1,0:T(8,128)(2,1)S(1)}, bf16[512,2048]{1,0:T(8,128)(2,1)S(1)}, bf16[512,2048]{1,0:T(8,128)(2,1)}) fusion(f32[512,4096]{1,0:T(8,128)} %fusion.79, f32[64,8,16,128]{3,2,1,0:T(8,128)S(1)} %bitcast.155, bf16[512,1024]{1,0:T(8,128)(2,1)} %all-gather.15.cloned.1.call-done, ...), kind=kOutput, calls=%fused_computation.11 | convolution fusion | flops 2166358016 | bytes 24117252 | tf_op jit(solution)/shard_map/dot_general | solution.py:194
  259.0 5.5 fusion.15
  264.7 6.1 %fusion.16 = bf16[512,1024]{1,0:T(8,128)(2,1)} fusion(bf16[512,2048]{1,0:T(8,128)(2,1)} %get-tuple-element.99, bf16[2048,2048]{0,1:T(8,128)(2,1)} %constant_dynamic-update-slice_fusion, s32[]{:T(128)S(6)} %select_n.42), kind=kOutput, calls=%fused_computation.36 | convolution fusion | flops 2148007936 | bytes 7340036 | tf_op jit(solution)/shard_map/dot_general | solution.py:212
  271.0 20.4 %reduce-scatter.16.cloned.1.call-done = bf16[128,1024]{1,0:T(8,128)(2,1)} async-done(((bf16[512,1024]{1,0:T(8,128)(2,1)}), bf16[128,1024]{1,0:T(8,128)(2,1)}) %reduce-scatter.16.cloned.1.call-update) | async-done | bytes 262160 | tf_op jit(solution)/shard_map/reduce_scatter | solution.py:203
  293.6 26.4 %reduce-scatter.14.cloned.1.call-done = bf16[128,1024]{1,0:T(8,128)(2,1)} async-done(((bf16[512,1024]{1,0:T(8,128)(2,1)}), bf16[128,1024]{1,0:T(8,128)(2,1)}) %reduce-scatter.14.cloned.1.call-update) | async-done | bytes 262160 | tf_op jit(solution)/shard_map/reduce_scatter | solution.py:215
  320.1 2.5 fusion.76
  322.6 26.6 %all-gather.17.cloned.1.call-done = bf16[512,1024]{1,0:T(8,128)(2,1)} async-done(((bf16[128,1024]{1,0:T(8,128)(2,1)}), bf16[512,1024]{1,0:T(8,128)(2,1)}) %all-gather.17.cloned.1.call-update) | async-done | bytes 1048592 | tf_op jit(solution)/shard_map/all_gather | solution.py:228
  352.1 3.8 fusion.2
  360.4 1.9 convolution_convert_fusion.2
  364.1 6.4 %convert_bitcast_fusion = bf16[1024,2048]{0,1:T(8,128)(2,1)} fusion(bf16[512,2048]{1,0:T(8,128)(2,1)} %get-tuple-element.99, bf16[512,1024]{1,0:T(8,128)(2,1)} %all-gather.15.cloned.1.call-done), kind=kOutput, calls=%fused_computation.9 | convolution fusion | flops 2149580800 | bytes 7340032 | tf_op jit(solution)/shard_map/dot_general | solution.py:206
  370.5 6.5 %copy.120 = bf16[1024,2048]{1,0:T(8,128)(2,1)} copy(bf16[1024,2048]{0,1:T(8,128)(2,1)} %convert_bitcast_fusion) | data formatting | bytes 8388608
  378.3 9.0 %convolution_convert_fusion = bf16[1024,4096]{1,0:T(8,128)(2,1)} fusion(bf16[512,1024]{1,0:T(8,128)(2,1)S(1)} %copy-done.42, bf16[512,2048]{1,0:T(8,128)(2,1)} %copy-done.44, bf16[512,2048]{1,0:T(8,128)(2,1)} %copy-done.43), kind=kOutput, calls=%fused_computation | convolution fusion | flops 4307550208 | bytes 13631488 | tf_op jit(solution)/shard_map/dot_general | solution.py:209
  389.2 40.1 %psum.7 = f32[2,1024]{1,0:T(2,128)S(1)} all-reduce(f32[2,1024]{1,0:T(2,128)S(1)} %pad_maximum_fusion.14), channel_id=1, replica_groups=mesh['dp'=8,'tensor'=4] {'dp','tensor'}, use_global_device_ids=true, to_apply=%region_13.14 | all-reduce | flops 2048 | bytes 16384 | tf_op jit(solution)/shard_map/psum | solution.py:276
  429.9 2.0 fusion.37
  435.0 47.4 %reduce-scatter.24.cloned.1.call-done = bf16[128,2048]{1,0:T(8,128)(2,1)} async-done(((bf16[1024,2048]{1,0:T(8,128)(2,1)}), bf16[128,2048]{1,0:T(8,128)(2,1)}) %reduce-scatter.24.cloned.1.call-update) | async-done | bytes 524304
  484.0 4.2 multiply_subtract_fusion.1
  488.1 69.2 %reduce-scatter.20.cloned.1.call-done = bf16[128,4096]{1,0:T(8,128)(2,1)} async-done(((bf16[1024,4096]{1,0:T(8,128)(2,1)}), bf16[128,4096]{1,0:T(8,128)(2,1)}) %reduce-scatter.20.cloned.1.call-update) | async-done | bytes 1048592 | tf_op jit(solution)/shard_map/reduce_scatter | solution.py:220
  560.6 4.9 multiply_subtract_fusion
  (192 shorter events, 59.6 us)
Async XLA Ops:
  7.2 43.0 %all-gather.7.cloned.1.call-start = ((), (), s32[]{:S(2)}) async-start(), calls=%async_computation.7 | async-start | bytes 1310720 | tf_op jit(solution)/shard_map/all_gather | solution.py:156
  21.7 56.1 %all-gather.9.cloned.1.call-start = ((), (), s32[]{:S(2)}) async-start(), calls=%async_computation.8 | async-start | bytes 1769472 | tf_op jit(solution)/shard_map/all_gather | solution.py:146
  24.6 89.9 %reduce-scatter.12.cloned.1.call-start = ((), (), s32[]{:S(2)}) async-start(), calls=%async_computation.9 | async-start | bytes 1310720 | tf_op jit(solution)/shard_map/reduce_scatter | solution.py:175
  24.8 57.5 %copy-start.8 = (pred[512,512]{0,1:T(8,128)(4,1)}, pred[512,512]{0,1:T(8,128)(4,1)S(1)}, u32[]{:S(2)}) copy-start(pred[512,512]{0,1:T(8,128)(4,1)S(1)} %iota_compare_fusion) | copy-start | bytes 786436
  80.2 3.0 copy-start.5
  83.3 31.1 %copy-start.1 = (f32[128,1024]{1,0:T(8,128)S(1)}, f32[128,1024]{1,0:T(8,128)}, u32[]{:S(2)}) copy-start(f32[128,1024]{1,0:T(8,128)} %param.19) | copy-start | bytes 1572868
  87.0 139.5 %all-gather.11.cloned.1.call-start = ((), (), s32[]{:S(2)}) async-start(), calls=%async_computation.10 | async-start | bytes 1310720 | tf_op jit(solution)/shard_map/all_gather | solution.py:180
  117.5 109.1 %all-gather.13.cloned.1.call-start = ((), (), s32[]{:S(2)}) async-start(), calls=%async_computation.11 | async-start | bytes 9437184 | tf_op jit(solution)/shard_map/all_gather | solution.py:157
  120.1 124.6 %all-gather.15.cloned.1.call-start = ((), (), s32[]{:S(2)}) async-start(), calls=%async_computation.13 | async-start | bytes 1310720 | tf_op jit(solution)/shard_map/all_gather | solution.py:166
  122.4 8.4 %collective-permute-start = (bf16[128,2048]{0,1:T(8,128)(2,1)}, bf16[128,2048]{0,1:T(8,128)(2,1)S(1)}, u32[]{:S(2)}, u32[]{:S(2)}) collective-permute-start(bf16[128,2048]{0,1:T(8,128)(2,1)} %bitcast.146), channel_id=1, source_target_pairs={{0,28},{4,0},{8,4},{12,8},{16,12},{20,16},{24,20},{28,24},{1,29},{... | collective-permute-start | bytes 1572872 | tf_op jit(solution)/shard_map/ppermute | solution.py:162
  131.6 9.8 %collective-permute-start.1 = (bf16[128,2048]{0,1:T(8,128)(2,1)S(1)}, bf16[128,2048]{0,1:T(8,128)(2,1)S(1)}, u32[]{:S(2)}, u32[]{:S(2)}) collective-permute-start(bf16[128,2048]{0,1:T(8,128)(2,1)S(1)} %collective-permute-done), channel_id=1, source_target_pairs={{0,28},{4,0},{8,4},{12,8},{16,12},{20,16},{24,20},{28,24},{1,29},{... | collective-permute-start | bytes 1572872 | tf_op jit(solution)/shard_map/ppermute | solution.py:162
  142.2 9.9 %collective-permute-start.2 = (bf16[128,2048]{0,1:T(8,128)(2,1)S(1)}, bf16[128,2048]{0,1:T(8,128)(2,1)S(1)}, u32[]{:S(2)}, u32[]{:S(2)}) collective-permute-start(bf16[128,2048]{0,1:T(8,128)(2,1)S(1)} %collective-permute-done.1), channel_id=1, source_target_pairs={{0,28},{4,0},{8,4},{12,8},{16,12},{20,16},{24,20},{28,24},{1,29},{... | collective-permute-start | bytes 1572872 | tf_op jit(solution)/shard_map/ppermute | solution.py:162
  152.9 18.1 %collective-permute-start.3 = (bf16[128,2048]{0,1:T(8,128)(2,1)S(1)}, bf16[128,2048]{0,1:T(8,128)(2,1)}, u32[]{:S(2)}, u32[]{:S(2)}) collective-permute-start(bf16[128,2048]{0,1:T(8,128)(2,1)S(1)} %collective-permute-done.2), channel_id=1, source_target_pairs={{0,28},{4,0},{8,4},{12,8},{16,12},{20,16},{24,20},{28,24},{1,29},{... | collective-permute-start | bytes 1572872 | tf_op jit(solution)/shard_map/ppermute | solution.py:162
  171.0 14.2 %collective-permute-start.4 = (bf16[128,2048]{0,1:T(8,128)(2,1)}, bf16[128,2048]{0,1:T(8,128)(2,1)}, u32[]{:S(2)}, u32[]{:S(2)}) collective-permute-start(bf16[128,2048]{0,1:T(8,128)(2,1)} %collective-permute-done.3), channel_id=1, source_target_pairs={{0,28},{4,0},{8,4},{12,8},{16,12},{20,16},{24,20},{28,24},{1,29},{... | collective-permute-start | bytes 1572872 | tf_op jit(solution)/shard_map/ppermute | solution.py:162
  175.8 115.6 %reduce-scatter.16.cloned.1.call-start = ((), (), s32[]{:S(2)}) async-start(), calls=%async_computation.14 | async-start | bytes 1310720 | tf_op jit(solution)/shard_map/reduce_scatter | solution.py:203
  178.8 38.4 %copy-start.3 = (bf16[16,128,128]{1,2,0:T(8,128)(2,1)S(1)}, bf16[16,128,128]{1,2,0:T(8,128)(2,1)}, u32[]{:S(2)}) copy-start(bf16[16,128,128]{1,2,0:T(8,128)(2,1)} %copy.94) | copy-start | bytes 1572868
  180.9 37.2 %copy-start.11 = (bf16[128,2048]{0,1:T(8,128)(2,1)S(1)}, bf16[128,2048]{0,1:T(8,128)(2,1)}, u32[]{:S(2)}) copy-start(bf16[128,2048]{0,1:T(8,128)(2,1)} %copy-done.10) | copy-start | bytes 1572868
  185.3 21.2 %collective-permute-start.5 = (bf16[128,2048]{0,1:T(8,128)(2,1)}, bf16[128,2048]{0,1:T(8,128)(2,1)S(1)}, u32[]{:S(2)}, u32[]{:S(2)}) collective-permute-start(bf16[128,2048]{0,1:T(8,128)(2,1)} %collective-permute-done.4), channel_id=1, source_target_pairs={{0,28},{4,0},{8,4},{12,8},{16,12},{20,16},{24,20},{28,24},{1,29},{... | collective-permute-start | bytes 1572872 | tf_op jit(solution)/shard_map/ppermute | solution.py:162
  190.0 29.0 %copy-start.13 = (bf16[128,2048]{0,1:T(8,128)(2,1)S(1)}, bf16[128,2048]{0,1:T(8,128)(2,1)}, u32[]{:S(2)}) copy-start(bf16[128,2048]{0,1:T(8,128)(2,1)} %copy-done.12) | copy-start | bytes 1572868
  192.1 27.9 %copy-start.15 = (bf16[128,2048]{0,1:T(8,128)(2,1)S(1)}, bf16[128,2048]{0,1:T(8,128)(2,1)}, u32[]{:S(2)}) copy-start(bf16[128,2048]{0,1:T(8,128)(2,1)} %copy-done.14) | copy-start | bytes 1572868
  206.4 9.9 %collective-permute-start.6 = (bf16[128,2048]{0,1:T(8,128)(2,1)S(1)}, bf16[128,2048]{0,1:T(8,128)(2,1)S(1)}, u32[]{:S(2)}, u32[]{:S(2)}) collective-permute-start(bf16[128,2048]{0,1:T(8,128)(2,1)S(1)} %collective-permute-done.5), channel_id=1, source_target_pairs={{0,28},{4,0},{8,4},{12,8},{16,12},{20,16},{24,20},{28,24},{1,29},{... | collective-permute-start | bytes 1572872 | tf_op jit(solution)/shard_map/ppermute | solution.py:162
  244.7 14.4 %slice-start = ((s8[8388608]{0:T(1024)(128)(4,1)}), s8[4194304]{0:T(1024)(128)(4,1)S(1)}, s32[]{:S(2)}) async-start(s8[8388608]{0:T(1024)(128)(4,1)} %bitcast.181), calls=%async_computation.20 | async-start | bytes 8388608
  246.9 12.1 %slice-start.1 = ((s8[8388608]{0:T(1024)(128)(4,1)}), s8[4194304]{0:T(1024)(128)(4,1)S(1)}, s32[]{:S(2)}) async-start(s8[8388608]{0:T(1024)(128)(4,1)} %bitcast.181), calls=%async_computation.21 | async-start | bytes 8388608
  264.5 55.5 %reduce-scatter.14.cloned.1.call-start = ((), (), s32[]{:S(2)}) async-start(), calls=%async_computation.12 | async-start | bytes 1310720 | tf_op jit(solution)/shard_map/reduce_scatter | solution.py:215
  270.9 78.3 %all-gather.17.cloned.1.call-start = ((), (), s32[]{:S(2)}) async-start(), calls=%async_computation.15 | async-start | bytes 1310720 | tf_op jit(solution)/shard_map/all_gather | solution.py:228
  322.6 65.0 %reduce-scatter.18.cloned.1.call-start = ((), (), s32[]{:S(2)}) async-start(), calls=%async_computation.16 | async-start | bytes 1310720 | tf_op jit(solution)/shard_map/reduce_scatter | solution.py:256
  352.1 3.8 copy-start.27
  352.1 3.8 copy-start.29
  352.1 4.3 copy-start.22
  352.1 4.3 copy-start.24
  359.9 72.0 %reduce-scatter.22.cloned.1.call-start = ((), (), s32[]{:S(2)}) async-start(), calls=%async_computation.18 | async-start | bytes 1769472
  364.1 118.3 %reduce-scatter.24.cloned.1.call-start = ((), (), s32[]{:S(2)}) async-start(), calls=%async_computation.19 | async-start | bytes 4718592
  377.1 180.3 %reduce-scatter.20.cloned.1.call-start = ((), (), s32[]{:S(2)}) async-start(), calls=%async_computation.17 | async-start | bytes 9437184 | tf_op jit(solution)/shard_map/reduce_scatter | solution.py:220
  387.4 41.9 %copy-start.38 = (f32[2,128]{1,0:T(2,128)S(1)}, f32[2,128]{1,0:T(2,128)}, u32[]{:S(2)}) copy-start(f32[2,128]{1,0:T(2,128)} %param.23) | copy-start | bytes 3076
  387.4 41.9 %copy-start.39 = (f32[2,128]{1,0:T(2,128)S(1)}, f32[2,128]{1,0:T(2,128)}, u32[]{:S(2)}) copy-start(f32[2,128]{1,0:T(2,128)} %param.28) | copy-start | bytes 3076
  387.4 41.9 %copy-start.40 = (f32[2,128]{1,0:T(2,128)S(1)}, f32[2,128]{1,0:T(2,128)}, u32[]{:S(2)}) copy-start(f32[2,128]{1,0:T(2,128)} %param.29) | copy-start | bytes 3076
  387.4 42.5 %copy-start.16 = (f32[128,1024]{1,0:T(8,128)S(1)}, f32[128,1024]{1,0:T(8,128)}, u32[]{:S(2)}) copy-start(f32[128,1024]{1,0:T(8,128)} %get-tuple-element.94) | copy-start | bytes 1572868
  387.4 42.5 %copy-start.41 = (f32[128]{0:T(128)S(1)}, f32[128]{0:T(128)}, u32[]{:S(2)}) copy-start(f32[128]{0:T(128)} %get-tuple-element.113) | copy-start | bytes 1540
  387.4 45.8 %copy-start.25 = (f32[2,128,128]{2,1,0:T(8,128)S(1)}, f32[2,128,128]{2,1,0:T(8,128)}, u32[]{:S(2)}) copy-start(f32[2,128,128]{2,1,0:T(8,128)} %param.25) | copy-start | bytes 393220
  387.4 45.8 %copy-start.32 = (f32[2,128,128]{2,1,0:T(8,128)S(1)}, f32[2,128,128]{2,1,0:T(8,128)}, u32[]{:S(2)}) copy-start(f32[2,128,128]{2,1,0:T(8,128)} %param.32) | copy-start | bytes 393220
  387.4 45.8 %copy-start.33 = (f32[2,128,128]{2,1,0:T(8,128)S(1)}, f32[2,128,128]{2,1,0:T(8,128)}, u32[]{:S(2)}) copy-start(f32[2,128,128]{2,1,0:T(8,128)} %param.33) | copy-start | bytes 393220
  387.5 46.5 %copy-start.19 = (f32[4,128,128]{2,1,0:T(8,128)S(1)}, f32[4,128,128]{2,1,0:T(8,128)}, u32[]{:S(2)}) copy-start(f32[4,128,128]{2,1,0:T(8,128)} %param.24) | copy-start | bytes 786436
  387.5 46.5 %copy-start.30 = (f32[4,128,128]{2,1,0:T(8,128)S(1)}, f32[4,128,128]{2,1,0:T(8,128)}, u32[]{:S(2)}) copy-start(f32[4,128,128]{2,1,0:T(8,128)} %param.30) | copy-start | bytes 786436
  387.5 46.5 %copy-start.31 = (f32[4,128,128]{2,1,0:T(8,128)S(1)}, f32[4,128,128]{2,1,0:T(8,128)}, u32[]{:S(2)}) copy-start(f32[4,128,128]{2,1,0:T(8,128)} %param.31) | copy-start | bytes 786436
  429.9 54.0 %copy-start.4 = (f32[16,128,128]{2,1,0:T(8,128)S(1)}, f32[16,128,128]{2,1,0:T(8,128)}, u32[]{:S(2)}) copy-start(f32[16,128,128]{2,1,0:T(8,128)} %param.27) | copy-start | bytes 3145732
  484.0 4.2 copy-start.6
  557.4 2.5 copy-start.17
  557.4 3.2 copy-start.18
  (19 other events, 27.8 us)
Sparse Core Ops, SparseCore 0:
  21.9 28.2 all-gather.6
  52.6 25.1 all-gather.8
  87.2 27.2 reduce-scatter.11
  117.6 26.4 all-gather.10
  146.4 68.1 all-gather.12
  216.6 28.0 all-gather.14
  264.6 26.6 reduce-scatter.15
  294.2 25.7 reduce-scatter.13
  322.7 26.4 all-gather.16
  360.0 26.6 reduce-scatter.17
  390.6 37.0 reduce-scatter.21
  430.9 51.4 reduce-scatter.23
  485.9 71.4 reduce-scatter.19
